TPU v7x, 32 devices: a whole 2x2x4 slice. The times are simulated.
32 devices in a mesh: fsdp: 4 (over y, x), rep: 8 (over z, core).
Axes of the slice: x: 2, y: 2, z: 4, core: 2. Of those that a mesh axis runs over, the one named last changes fastest.
Arguments:
- tokens: bfloat16 [64, 256, 384], P(('fsdp', 'rep')), may hold values from -6 to 6
- conditions: bfloat16 [64, 384], P(('fsdp', 'rep')), may hold values from -6 to 6
- assignment: int32 [64], P(('fsdp', 'rep')), may hold values from 0 to 63, each once
- params: float32 [2654208], P('fsdp')
- momentum: float32 [2654208], P('fsdp'), may hold values from -24 to 24
- cotangent: bfloat16 [64, 256, 384], P(('fsdp', 'rep')), may hold values from -6 to 6
Outputs:
- blended: bfloat16 [64, 256, 384], P(('fsdp', 'rep'))
- grad_tokens: float32 [64, 256, 384], P(('fsdp', 'rep'))
- grad_params: float32 [2654208], P('fsdp')
- new_params: float32 [2654208], P('fsdp')
- new_momentum: float32 [2654208], P('fsdp')
Inputs may be any that keep to these rules, and one draw needn't show every extreme that they name: assignment is a permutation of the latent numbers.
All inputs are finite; a program needn't handle non-finite values.
Results may differ from a plain program's by a relative error of at most 0.014.
The roundings to bfloat16 on the way count: a program that leaves them out, or rounds other values in their place, can miss the bound.
Values may be sent and summed in bfloat16 or wider, within the bound.
No kernel may reach another device: no remote copies, remote signals or barrier semaphores. Data moves between devices by JAX's collectives and lax.ppermute only.
A program may use at most 192 MiB of HBM per device.

v0:
```python
import math
import jax
import jax.numpy as jnp
from jax import lax
from jax.sharding import PartitionSpec as P

D = 384
HEADS = 6
HD = 64
FF = 1536
SEQ = 256
NS_ITERS = 3
LN_EPSILON = 1e-06
MOMENTUM_RATE = 0.95
LEARN_RATE = 0.2
COEFF_A = 3.4445
COEFF_B = -4.775
COEFF_C = 2.0315


def matrix_shapes():
    return [(D, 6 * D), (D, 3 * D), (D, D), (D, FF), (FF, D)]


def unpack(flat_vec):
    pieces = []
    offset = 0
    for rows_count, cols_count in matrix_shapes():
        pieces.append(
            flat_vec[offset : offset + rows_count * cols_count].reshape(rows_count, cols_count)
        )
        offset += rows_count * cols_count
    return pieces


def matmul(lhs_array, rhs_array):
    return jnp.dot(lhs_array, rhs_array, preferred_element_type=jnp.float32)


def contract(pattern, lhs_array, rhs_array):
    return jnp.einsum(pattern, lhs_array, rhs_array, preferred_element_type=jnp.float32)


def modulate(hidden, shifts, scales):
    center = jnp.mean(hidden, axis=-1, keepdims=True)
    spread = jnp.mean(jnp.square(hidden - center), axis=-1, keepdims=True)
    return (hidden - center) * lax.rsqrt(spread + LN_EPSILON) * (1.0 + scales) + shifts


def gelu_tanh(values_in):
    return jax.nn.gelu(values_in, approximate=True)


def orthogonalize(matrix):
    flipped = matrix.shape[0] > matrix.shape[1]
    current = matrix.T if flipped else matrix
    current = current / (jnp.sqrt(jnp.sum(current * current)) + 1e-07)
    for newton_step in range(NS_ITERS):
        square = jnp.dot(current, current.T, precision=lax.Precision.HIGHEST)
        polynomial = COEFF_B * square + COEFF_C * jnp.dot(
            square, square, precision=lax.Precision.HIGHEST
        )
        current = COEFF_A * current + jnp.dot(polynomial, current, precision=lax.Precision.HIGHEST)
    return current.T if flipped else current


def update_scale(rows_count, cols_count):
    return LEARN_RATE * 0.2 * math.sqrt(max(rows_count, cols_count))


def scaled_update(matrix, factor):
    return (factor * orthogonalize(matrix)).reshape(-1)


def empty_update(matrix, factor):
    return jnp.zeros((matrix.shape[0] * matrix.shape[1],), jnp.float32)


def forward_pass(tokens, cond_rows, weights):
    adaln_weight, qkv_weight, out_weight, up_weight, down_weight = weights
    batch_size = tokens.shape[0]
    row_count = batch_size * SEQ
    silu_cond = jax.nn.silu(cond_rows.astype(jnp.float32)).astype(jnp.bfloat16)
    modulation = matmul(silu_cond, adaln_weight).reshape(batch_size, 6, 1, D)
    mod_parts = tuple((modulation[:, position] for position in range(6)))
    shift_attn, scale_attn, gate_attn, shift_mlp, scale_mlp, gate_mlp = mod_parts
    residual = tokens.astype(jnp.float32)
    attn_input = modulate(residual, shift_attn, scale_attn).astype(jnp.bfloat16)
    qkv_all = matmul(attn_input.reshape(row_count, D), qkv_weight).astype(jnp.bfloat16)
    qkv_heads = qkv_all.reshape(batch_size, SEQ, 3, HEADS, HD).transpose(2, 0, 3, 1, 4)
    queries, key_vecs, value_vecs = (qkv_heads[0], qkv_heads[1], qkv_heads[2])
    scores = contract("bhqd,bhkd->bhqk", queries, key_vecs) * HD ** (-0.5)
    log_total = jax.nn.logsumexp(scores, axis=-1, keepdims=True)
    attn_probs = jnp.exp(scores - log_total).astype(jnp.bfloat16)
    attn_mixed = contract("bhqk,bhkd->bhqd", attn_probs, value_vecs).astype(jnp.bfloat16)
    attn_mixed = attn_mixed.transpose(0, 2, 1, 3).reshape(row_count, D)
    attn_out = matmul(attn_mixed, out_weight).reshape(batch_size, SEQ, D)
    after_attn = residual + gate_attn * attn_out
    mlp_input = (
        modulate(after_attn, shift_mlp, scale_mlp).astype(jnp.bfloat16).reshape(row_count, D)
    )
    pre_act = matmul(mlp_input, up_weight)
    activated = gelu_tanh(pre_act).astype(jnp.bfloat16)
    mlp_out = matmul(activated, down_weight).reshape(batch_size, SEQ, D)
    blended = (after_attn + gate_mlp * mlp_out).astype(jnp.bfloat16)
    kept_state = (
        silu_cond,
        mod_parts,
        residual,
        attn_input,
        queries,
        key_vecs,
        value_vecs,
        log_total,
        attn_mixed,
        attn_out,
        after_attn,
        mlp_input,
        pre_act,
        activated,
        mlp_out,
    )
    return (blended, kept_state)


def backward_pass(kept_state, weights, cotangent):
    (
        silu_cond,
        mod_parts,
        residual,
        attn_input,
        queries,
        key_vecs,
        value_vecs,
        log_total,
        attn_mixed,
        attn_out,
        after_attn,
        mlp_input,
        pre_act,
        activated,
        mlp_out,
    ) = kept_state
    adaln_weight, qkv_weight, out_weight, up_weight, down_weight = weights
    shift_attn, scale_attn, gate_attn, shift_mlp, scale_mlp, gate_mlp = mod_parts
    batch_size = cotangent.shape[0]
    row_count = batch_size * SEQ
    upstream = cotangent.astype(jnp.float32)
    grad_gate_mlp = jnp.sum(upstream * mlp_out, axis=1, keepdims=True)
    grad_mlp_out = (upstream * gate_mlp).astype(jnp.bfloat16).reshape(row_count, D)
    grad_down = matmul(activated.T, grad_mlp_out)
    grad_act = matmul(grad_mlp_out, down_weight.T)
    grad_pre = jax.vjp(gelu_tanh, pre_act)[1](grad_act)[0].astype(jnp.bfloat16)
    grad_up = matmul(mlp_input.T, grad_pre)
    grad_mlp_in = matmul(grad_pre, up_weight.T).reshape(batch_size, SEQ, D)
    grad_after, grad_shift_mlp, grad_scale_mlp = jax.vjp(
        modulate, after_attn, shift_mlp, scale_mlp
    )[1](grad_mlp_in)
    grad_after = upstream + grad_after
    grad_gate_attn = jnp.sum(grad_after * attn_out, axis=1, keepdims=True)
    grad_attn_out = (grad_after * gate_attn).astype(jnp.bfloat16).reshape(row_count, D)
    grad_outw = matmul(attn_mixed.T, grad_attn_out)
    grad_mixed = matmul(grad_attn_out, out_weight.T).astype(jnp.bfloat16)
    grad_mixed = grad_mixed.reshape(batch_size, SEQ, HEADS, HD).transpose(0, 2, 1, 3)
    scores = contract("bhqd,bhkd->bhqk", queries, key_vecs) * HD ** (-0.5)
    probs_full = jnp.exp(scores - log_total)
    grad_values = contract("bhqk,bhqd->bhkd", probs_full.astype(jnp.bfloat16), grad_mixed)
    grad_probs = contract("bhqd,bhkd->bhqk", grad_mixed, value_vecs)
    row_dots = jnp.sum(probs_full * grad_probs, axis=-1, keepdims=True)
    grad_scores = (probs_full * (grad_probs - row_dots) * HD ** (-0.5)).astype(jnp.bfloat16)
    grad_queries = contract("bhqk,bhkd->bhqd", grad_scores, key_vecs)
    grad_keys = contract("bhqk,bhqd->bhkd", grad_scores, queries)
    grad_qkv = jnp.stack([grad_queries, grad_keys, grad_values], axis=0).transpose(1, 3, 0, 2, 4)
    grad_qkv = grad_qkv.reshape(row_count, 3 * D).astype(jnp.bfloat16)
    grad_qkvw = matmul(attn_input.reshape(row_count, D).T, grad_qkv)
    grad_attn_in = matmul(grad_qkv, qkv_weight.T).reshape(batch_size, SEQ, D)
    grad_resid, grad_shift_attn, grad_scale_attn = jax.vjp(
        modulate, residual, shift_attn, scale_attn
    )[1](grad_attn_in)
    grad_tokens = grad_after + grad_resid
    grad_mod = jnp.concatenate(
        [
            grad_shift_attn,
            grad_scale_attn,
            grad_gate_attn,
            grad_shift_mlp,
            grad_scale_mlp,
            grad_gate_mlp,
        ],
        axis=1,
    )
    grad_mod = grad_mod.reshape(batch_size, 6 * D).astype(jnp.bfloat16)
    grad_adaln = matmul(silu_cond.T, grad_mod)
    flat_grads = jnp.concatenate(
        [
            grad_adaln.reshape(-1),
            grad_qkvw.reshape(-1),
            grad_outw.reshape(-1),
            grad_up.reshape(-1),
            grad_down.reshape(-1),
        ]
    )
    return (grad_tokens, flat_grads)


def on_device(tokens, conditions, assignment, params, momentum, cotangent):
    cond_table = lax.all_gather(conditions, ("fsdp", "rep"), axis=0, tiled=True)
    cond_rows = jnp.take(cond_table, assignment, axis=0)
    low_params = params.astype(jnp.bfloat16)
    gathered = lax.all_gather(low_params, "fsdp", axis=0, tiled=True)
    blended, kept_state = forward_pass(tokens, cond_rows, unpack(gathered))
    back_flat = lax.all_gather(low_params, "fsdp", axis=0, tiled=True)
    grad_tokens, flat_grads = backward_pass(kept_state, unpack(back_flat), cotangent)
    group_part = lax.psum_scatter(flat_grads, "fsdp", scatter_dimension=0, tiled=True)
    full_grad = lax.psum(group_part, "rep")
    new_momentum = MOMENTUM_RATE * momentum + full_grad
    whole_mom = lax.all_gather(new_momentum, "fsdp", axis=0, tiled=True)
    fsdp_rank = lax.axis_index("fsdp")
    group_size = lax.axis_size("fsdp")
    shard_len = params.shape[0]
    updates = []
    offset = 0
    for rows_count, cols_count in matrix_shapes():
        length = rows_count * cols_count
        piece = whole_mom[offset : offset + length].reshape(rows_count, cols_count)
        factor = jnp.float32(update_scale(rows_count, cols_count))
        owner_rank = (offset // shard_len + group_size // 2) % group_size
        updates.append(
            lax.cond(fsdp_rank == owner_rank, scaled_update, empty_update, piece, factor)
        )
        offset += length
    local_update = lax.psum_scatter(
        jnp.concatenate(updates), "fsdp", scatter_dimension=0, tiled=True
    )
    new_params = params - local_update
    return (blended, grad_tokens, full_grad, new_params, new_momentum)


def solution(mesh):
    in_specs = (
        P(("fsdp", "rep"), None, None),
        P(("fsdp", "rep"), None),
        P(("fsdp", "rep")),
        P("fsdp"),
        P("fsdp"),
        P(("fsdp", "rep"), None, None),
    )
    out_specs = (
        P(("fsdp", "rep"), None, None),
        P(("fsdp", "rep"), None, None),
        P("fsdp"),
        P("fsdp"),
        P("fsdp"),
    )
    return jax.shard_map(
        on_device, mesh=mesh, in_specs=in_specs, out_specs=out_specs, check_vma=False
    )
```

profile of v0, /device:TPU:0, one launch (start us, length us, event | category | flops | bytes accessed | tf_op | source)
XLA Modules:
  0.0 911.6 jit_solution(14796318998570174122)
XLA Ops:
  7.2 3.0 convert_element_type.90
  10.3 44.1 %all-gather = bf16[32,2,384]{2,1,0:T(2,128)(2,1)S(1)} all-gather(bf16[1,2,384]{2,1,0:T(2,128)(2,1)S(1)} %bitcast.245), channel_id=1, replica_groups=mesh['fsdp'=4,'rep'=8] {'fsdp','rep'}, dimensions={0}, use_global_device_ids=true | all-gather | bytes 50688 | tf_op jit(solution)/shard_map/all_gather | solution.py:207
  55.5 19.7 %all-gather.4.cloned.1.call-done = bf16[2654208]{0:T(1024)(128)(2,1)} async-done(((bf16[663552]{0:T(1024)(128)(2,1)}), bf16[2654208]{0:T(1024)(128)(2,1)}) %all-gather.4.cloned.1.call-update) | async-done | bytes 5308432 | tf_op jit(solution)/shard_map/all_gather | solution.py:210
  92.5 3.0 slice.157
  95.5 2.8 copy.42
  108.5 2.8 fusion.36
  129.6 3.3 fusion.73
  132.9 5.2 fusion.49
  138.1 5.1 fusion.52
  153.1 3.4 reshape.341
  167.0 4.1 constant_dynamic-update-slice_fusion.6
  179.8 205.9 %all-reduce.8.cloned.1.call-done = f32[2654208]{0:T(1024)} async-done(((f32[2654208]{0:T(1024)}), f32[2654208]{0:T(1024)}) %all-reduce.8.cloned.1.call-update) | async-done | bytes 10616848
  385.8 3.4 dynamic-slice.1
  389.3 69.3 %all-reduce.6.cloned.1.call-done = f32[663552]{0:T(1024)} async-done(((f32[663552]{0:T(1024)}), f32[663552]{0:T(1024)}) %all-reduce.6.cloned.1.call-update) | async-done | bytes 2654224 | tf_op jit(solution)/shard_map/psum | solution.py:215
  458.5 3.6 multiply_add_fusion.3
  462.2 105.5 %all-gather.6.cloned.1.call-done = f32[2654208]{0:T(1024)} async-done(((f32[663552]{0:T(1024)}), f32[2654208]{0:T(1024)}) %all-gather.6.cloned.1.call-update) | async-done | bytes 10616848 | tf_op jit(solution)/shard_map/all_gather | solution.py:217
  567.7 9.3 %conditional.5 = (f32[884736]{0:T(1024)S(1)}) conditional(s32[]{:T(128)} %convert_element_type.110, () %tuple.38, f32[2654208]{0:T(1024)} %all-gather.6.cloned.1.call-done), branch_computations={%region_21.22_spmd, %region_22.24_spmd} | conditional | flops 26509787136 | bytes 63701028 | solution.py:229
  579.1 14.8 %conditional.6 = (f32[442368]{0:T(1024)S(1)}) conditional(s32[]{:T(128)} %convert_element_type.111, () %tuple.39, f32[2654208]{0:T(1024)} %all-gather.6.cloned.1.call-done), branch_computations={%region_24.25_spmd, %region_25.27_spmd} | conditional | flops 14274772992 | bytes 35389476 | solution.py:229
  595.3 15.7 %conditional.7 = (f32[147456]{0:T(1024)S(1)}) conditional(s32[]{:T(128)} %convert_element_type.112, () %tuple.40, f32[2654208]{0:T(1024)} %all-gather.6.cloned.1.call-done), branch_computations={%region_27.28_spmd, %region_28.30_spmd} | conditional | flops 6118096896 | bytes 16515108 | solution.py:229
  611.8 41.5 %conditional.8 = (f32[589824]{0:T(1024)S(1)}) conditional(s32[]{:T(128)} %convert_element_type.112, () %tuple.41, f32[2654208]{0:T(1024)} %all-gather.6.cloned.1.call-done), branch_computations={%region_30.31_spmd, %region_31.33_spmd} | conditional | flops 18353111040 | bytes 44826660 | solution.py:229
  611.8 2.9 multiply_reduce_fusion.3
  615.4 3.2 slice_divide_fusion.3
  621.1 4.0 fusion.109
  626.3 4.0 convolution_add_fusion.11
  630.3 4.2 fusion.110
  635.8 4.0 convolution_add_fusion.10
  639.8 4.0 fusion.111
  645.1 5.5 fusion.12
  655.0 10.3 %conditional.9 = (f32[589824]{0:T(1024)S(1)}) conditional(s32[]{:T(128)} %convert_element_type.113, () %tuple.42, f32[2654208]{0:T(1024)} %all-gather.6.cloned.1.call-done), branch_computations={%region_33.34_spmd, %region_34.36_spmd} | conditional | flops 18360188928 | bytes 110887024 | solution.py:229
  668.1 2.6 fusion.65
  670.7 228.7 %all-reduce.10.cloned.1.call-done = f32[2654208]{0:T(1024)} async-done(((f32[2654208]{0:T(1024)}), f32[2654208]{0:T(1024)}) %all-reduce.10.cloned.1.call-update) | async-done | bytes 10616848
  899.5 3.7 dynamic-slice_subtract_fusion
  (231 shorter events, 109.2 us)
Async XLA Ops:
  7.2 3.1 copy-start.55
  7.2 47.2 %copy-start.58 = (s32[2]{0:T(128)S(1)}, s32[2]{0:T(128)}, u32[]{:S(2)}) copy-start(s32[2]{0:T(128)} %param.18) | copy-start | bytes 28
  7.2 47.8 %copy-start.3 = (bf16[2,256,384]{2,1,0:T(8,128)(2,1)S(1)}, bf16[2,256,384]{2,1,0:T(8,128)(2,1)}, u32[]{:S(2)}) copy-start(bf16[2,256,384]{2,1,0:T(8,128)(2,1)} %param.16) | copy-start | bytes 1179652
  7.2 68.0 %all-gather.4.cloned.1.call-start = ((), (), s32[]{:S(2)}) async-start(), calls=%async_computation | async-start | bytes 6635520 | tf_op jit(solution)/shard_map/all_gather | solution.py:210
  10.3 375.5 %all-reduce.8.cloned.1.call-start = ((), (), s32[]{:S(2)}) async-start(), calls=%async_computation.3 | async-start | bytes 21233664
  55.0 43.3 %copy-start.46 = (bf16[2,384]{1,0:T(2,128)(2,1)}, bf16[2,384]{1,0:T(2,128)(2,1)S(1)}, u32[]{:S(2)}) copy-start(bf16[2,384]{1,0:T(2,128)(2,1)S(1)} %gather_fusion) | copy-start | bytes 4612
  55.2 44.3 %copy-start.34 = (f32[2,256]{1,0:T(2,128)}, f32[2,256]{1,0:T(2,128)S(1)}, u32[]{:S(2)}) copy-start(f32[2,256]{1,0:T(2,128)S(1)} %broadcast_multiply_fusion.2) | copy-start | bytes 6148
  55.5 25.6 %copy-start.42 = (f32[2,256]{1,0:T(2,128)}, f32[2,256]{1,0:T(2,128)S(1)}, u32[]{:S(2)}) copy-start(f32[2,256]{1,0:T(2,128)S(1)} %fusion.69) | copy-start | bytes 6148
  55.5 42.8 %copy-start.52 = (pred[2]{0:T(512)(128)(4,1)}, pred[2]{0:T(512)(128)(4,1)S(1)}, u32[]{:S(2)}) copy-start(pred[2]{0:T(512)(128)(4,1)S(1)} %compare_and_fusion) | copy-start | bytes 10
  55.5 44.0 %copy-start.44 = (f32[2,256]{1,0:T(2,128)}, f32[2,256]{1,0:T(2,128)S(1)}, u32[]{:S(2)}) copy-start(f32[2,256]{1,0:T(2,128)S(1)} %fusion.85) | copy-start | bytes 6148
  98.2 3.3 copy-start.15
  99.5 3.5 copy-start.37
  99.5 3.5 copy-start.39
  105.5 2.9 copy-start.20
  115.5 2.5 copy-start.14
  115.5 2.5 copy-start.25
  115.5 2.4 copy-start.38
  118.0 4.2 copy-start.32
  127.1 2.5 copy-start.22
  144.6 3.4 copy-start.21
  148.0 3.6 copy-start.2
  153.1 3.5 copy-start.13
  158.1 2.5 copy-start.17
  167.0 4.1 copy-start.10
  171.1 2.7 copy-start.8
  173.8 2.5 copy-start.7
  178.0 280.6 %all-reduce.6.cloned.1.call-start = ((), (), s32[]{:S(2)}) async-start(), calls=%async_computation.1 | async-start | bytes 5308416 | tf_op jit(solution)/shard_map/psum | solution.py:215
  389.2 69.3 %copy-start.23 = (f32[663552]{0:T(1024)S(1)}, f32[663552]{0:T(1024)}, u32[]{:S(2)}) copy-start(f32[663552]{0:T(1024)} %param.20) | copy-start | bytes 7962628
  389.2 178.5 %all-gather.6.cloned.1.call-start = ((), (), s32[]{:S(2)}) async-start(), calls=%async_computation.2 | async-start | bytes 13271040 | tf_op jit(solution)/shard_map/all_gather | solution.py:217
  462.1 437.3 %all-reduce.10.cloned.1.call-start = ((), (), s32[]{:S(2)}) async-start(), calls=%async_computation.4 | async-start | bytes 21233664
  666.8 232.6 %copy-start.5 = (f32[663552]{0:T(1024)S(1)}, f32[663552]{0:T(1024)}, u32[]{:S(2)}) copy-start(f32[663552]{0:T(1024)} %param.19) | copy-start | bytes 7962628
  899.5 3.7 copy-start.6
  (31 other events, 39.9 us)
Sparse Core Ops, SparseCore 0:
  10.4 64.7 all-gather.3
  178.1 207.6 all-reduce.7
  389.3 69.1 all-reduce.5
  462.2 105.4 all-gather.5
  667.0 232.4 all-reduce.9
where the time goes:
time: 916 us; the launch traced here: 912 us
  waiting for transfers between devices  629 us (69%)
  matrix products  80.4 us (9%)
  local copies, waits for them, and re-layouts  77.9 us (9%)
  blocking collectives  44.1 us (5%)
  loops' own time  36.2 us (4%)
  other arithmetic  28.1 us (3%)
  between operations  15.4 us (2%)
    unnamed x7, waiting for transfers between devices  435 us
    all_gather x1, waiting for transfers between devices, on_device(): whole_mom = lax.all_gather(new_momentum, 'fsdp', axis=0, tiled=True)  106 us
    psum x1, waiting for transfers between devices, on_device(): full_grad = lax.psum(group_part, 'rep')  69.3 us
    all_gather x1, blocking collectives, on_device(): cond_table = lax.all_gather(conditions, ('fsdp', 'rep'), axis=0, tiled=True)  44.1 us
    another operation x5, loops' own time, on_device(): lax.cond(fsdp_rank == owner_rank, scaled_update, empty_update, piece, fac...  36.2 us
    unnamed x133, local copies, waits for them, and re-layouts  26.7 us
    dot_general x14, matrix products, matmul(): return jnp.dot(lhs_array, rhs_array, preferred_element_type=jnp.float32)  22 us
    slice x14, local copies, waits for them, and re-layouts, unpack(): flat_vec[offset:offset + rows_count * cols_count]  20.3 us
  transfers between devices with their start and end apart: 5, of which 5 were waited for; matrix products, arithmetic and copies ran while one was open for 0% of the time, Pallas kernels for 0%

commit v1 on v0

--- a/solution.py
+++ b/solution.py
@@ -212,7 +212,7 @@
     back_flat = lax.all_gather(low_params, "fsdp", axis=0, tiled=True)
     grad_tokens, flat_grads = backward_pass(kept_state, unpack(back_flat), cotangent)
     group_part = lax.psum_scatter(flat_grads, "fsdp", scatter_dimension=0, tiled=True)
-    full_grad = lax.psum(group_part, "rep")
+    full_grad = jnp.sum(lax.all_gather(group_part, "rep"), 0)
     new_momentum = MOMENTUM_RATE * momentum + full_grad
     whole_mom = lax.all_gather(new_momentum, "fsdp", axis=0, tiled=True)
     fsdp_rank = lax.axis_index("fsdp")

time: 916 us -> 1090 us (1.19)
  waiting for transfers between devices: 629 us -> 738 us
  other arithmetic: 28.1 us -> 57.3 us
  local copies, waits for them, and re-layouts: 77.9 us -> 102 us
    all_gather x0 -> x1, waiting for transfers between devices: none -> 188 us  [on_device(): full_grad = jnp.sum(lax.all_gather(group_part, 'rep'), 0)]
    psum x1 -> x0, waiting for transfers between devices: 69.3 us -> none  [on_device(): full_grad = lax.psum(group_part, 'rep')]
    reduce_sum x0 -> x1, other arithmetic: none -> 29.4 us  [on_device(): full_grad = jnp.sum(lax.all_gather(group_part, 'rep'), 0)]
    all_gather x0 -> x1, local copies, waits for them, and re-layouts: none -> 17.9 us  [on_device(): full_grad = jnp.sum(lax.all_gather(group_part, 'rep'), 0)]
    slice x14 -> x13, local copies, waits for them, and re-layouts: 20.3 us -> 23.4 us  [unpack(): flat_vec[offset:offset + rows_count * cols_count]]
    unnamed x133 -> x136, local copies, waits for them, and re-layouts: 26.7 us -> 26 us
where the time goes in v1:
time: 1090 us; the launch traced here: 1080 us
  waiting for transfers between devices  738 us (68%)
  local copies, waits for them, and re-layouts  102 us (9%)
  matrix products  82.2 us (8%)
  other arithmetic  57.3 us (5%)
  loops' own time  44.3 us (4%)
  blocking collectives  44.1 us (4%)
  between operations  15.7 us (1%)
    unnamed x7, waiting for transfers between devices  426 us
    all_gather x1, waiting for transfers between devices, on_device(): full_grad = jnp.sum(lax.all_gather(group_part, 'rep'), 0)  188 us
    all_gather x1, waiting for transfers between devices, on_device(): whole_mom = lax.all_gather(new_momentum, 'fsdp', axis=0, tiled=True)  104 us
    another operation x5, loops' own time, on_device(): lax.cond(fsdp_rank == owner_rank, scaled_update, empty_update, piece, fac...  44.3 us
    all_gather x1, blocking collectives, on_device(): cond_table = lax.all_gather(conditions, ('fsdp', 'rep'), axis=0, tiled=True)  44.1 us
    reduce_sum x1, other arithmetic, on_device(): full_grad = jnp.sum(lax.all_gather(group_part, 'rep'), 0)  29.4 us
    unnamed x136, local copies, waits for them, and re-layouts  26 us
    dot_general x14, matrix products, matmul(): return jnp.dot(lhs_array, rhs_array, preferred_element_type=jnp.float32)  23.6 us
  transfers between devices with their start and end apart: 5, of which 5 were waited for; matrix products, arithmetic and copies ran while one was open for 0% of the time, Pallas kernels for 0%

profile of v1, /device:TPU:0, one launch (start us, length us, event | category | flops | bytes accessed | tf_op | source)
XLA Modules:
  0.0 1083.4 jit_solution(2894275211151539979)
XLA Ops:
  7.2 3.0 convert_element_type.90
  10.3 44.1 %all-gather.1 = bf16[32,2,384]{2,1,0:T(2,128)(2,1)S(1)} all-gather(bf16[1,2,384]{2,1,0:T(2,128)(2,1)S(1)} %bitcast.245), channel_id=1, replica_groups=mesh['fsdp'=4,'rep'=8] {'fsdp','rep'}, dimensions={0}, use_global_device_ids=true | all-gather | bytes 50688 | tf_op jit(solution)/shard_map/all_gather | solution.py:207
  55.5 19.7 %all-gather.6.cloned.1.call-done = bf16[2654208]{0:T(1024)(128)(2,1)} async-done(((bf16[663552]{0:T(1024)(128)(2,1)}), bf16[2654208]{0:T(1024)(128)(2,1)}) %all-gather.6.cloned.1.call-update) | async-done | bytes 5308432 | tf_op jit(solution)/shard_map/all_gather | solution.py:210
  89.6 3.6 slice.157
  129.2 3.3 fusion.73
  132.4 5.1 fusion.52
  137.6 5.2 fusion.49
  142.8 3.3 reshape.359
  158.4 4.6 reshape.337
  163.0 4.1 constant_dynamic-update-slice_fusion.6
  173.5 3.2 reshape.341
  188.1 205.9 %all-reduce.5.cloned.1.call-done = f32[2654208]{0:T(1024)} async-done(((f32[2654208]{0:T(1024)}), f32[2654208]{0:T(1024)}) %all-reduce.5.cloned.1.call-update) | async-done | bytes 10616848
  394.0 3.4 dynamic-slice.1
  397.7 187.5 %all-gather.10.cloned.1.call-done = f32[5308416]{0:T(1024)} async-done(((f32[663552]{0:T(1024)}), f32[5308416]{0:T(1024)}) %all-gather.10.cloned.1.call-update) | async-done | bytes 21233680 | tf_op jit(solution)/shard_map/all_gather | solution.py:215
  585.2 17.9 %reshape.351 = f32[8,663552]{1,0:T(8,128)} reshape(f32[5308416]{0:T(1024)} %all-gather.10.cloned.1.call-done) | data formatting | bytes 42467328 | tf_op jit(solution)/shard_map/all_gather | solution.py:215
  603.1 29.4 %reduce_sum.266 = f32[663552]{0:T(1024)S(1)} reduce(f32[8,663552]{1,0:T(8,128)} %reshape.351, f32[]{:T(128)} %constant.97.clone.1), dimensions={0}, to_apply=%region_20.21 | reduce | flops 4644864 | bytes 23887876 | tf_op jit(solution)/shard_map/reduce_sum | solution.py:215
  632.5 4.5 multiply_add_fusion.3
  637.1 104.3 %all-gather.8.cloned.1.call-done = f32[2654208]{0:T(1024)} async-done(((f32[663552]{0:T(1024)}), f32[2654208]{0:T(1024)}) %all-gather.8.cloned.1.call-update) | async-done | bytes 10616848 | tf_op jit(solution)/shard_map/all_gather | solution.py:217
  741.4 9.3 conditional.5
  752.8 14.7 %conditional.6 = (f32[442368]{0:T(1024)S(1)}) conditional(s32[]{:T(128)} %convert_element_type.111, () %tuple.39, f32[2654208]{0:T(1024)} %all-gather.8.cloned.1.call-done), branch_computations={%region_24.25_spmd, %region_25.27_spmd} | conditional | flops 14274772992 | bytes 35389476 | solution.py:229
  768.8 24.7 %conditional.7 = (f32[147456]{0:T(1024)S(1)}) conditional(s32[]{:T(128)} %convert_element_type.112, () %tuple.40, f32[2654208]{0:T(1024)} %all-gather.8.cloned.1.call-done), branch_computations={%region_27.28_spmd, %region_28.30_spmd} | conditional | flops 6118096896 | bytes 16515108 | solution.py:229
  794.4 41.5 %conditional.8 = (f32[589824]{0:T(1024)S(1)}) conditional(s32[]{:T(128)} %convert_element_type.112, () %tuple.41, f32[2654208]{0:T(1024)} %all-gather.8.cloned.1.call-done), branch_computations={%region_30.31_spmd, %region_31.33_spmd} | conditional | flops 18353111040 | bytes 44826660 | solution.py:229
  797.9 3.2 slice_divide_fusion.3
  803.6 4.0 fusion.109
  808.9 4.0 convolution_add_fusion.11
  812.9 4.4 fusion.110
  818.6 4.0 convolution_add_fusion.10
  822.6 4.0 fusion.111
  827.9 5.5 fusion.12
  837.5 9.8 conditional.9
  852.7 220.2 %all-reduce.7.cloned.1.call-done = f32[2654208]{0:T(1024)} async-done(((f32[2654208]{0:T(1024)}), f32[2654208]{0:T(1024)}) %all-reduce.7.cloned.1.call-update) | async-done | bytes 10616848
  1072.9 3.5 dynamic-slice_subtract_fusion
  (235 shorter events, 118.7 us)
Async XLA Ops:
  7.2 3.1 copy-start.57
  7.2 47.2 %copy-start.60 = (s32[2]{0:T(128)S(1)}, s32[2]{0:T(128)}, u32[]{:S(2)}) copy-start(s32[2]{0:T(128)} %param.18) | copy-start | bytes 28
  7.2 47.8 %copy-start.3 = (bf16[2,256,384]{2,1,0:T(8,128)(2,1)S(1)}, bf16[2,256,384]{2,1,0:T(8,128)(2,1)}, u32[]{:S(2)}) copy-start(bf16[2,256,384]{2,1,0:T(8,128)(2,1)} %param.16) | copy-start | bytes 1179652
  7.2 68.0 %all-gather.6.cloned.1.call-start = ((), (), s32[]{:S(2)}) async-start(), calls=%async_computation | async-start | bytes 6635520 | tf_op jit(solution)/shard_map/all_gather | solution.py:210
  10.3 383.8 %all-reduce.5.cloned.1.call-start = ((), (), s32[]{:S(2)}) async-start(), calls=%async_computation.3 | async-start | bytes 21233664
  55.0 40.4 %copy-start.49 = (bf16[2,384]{1,0:T(2,128)(2,1)}, bf16[2,384]{1,0:T(2,128)(2,1)S(1)}, u32[]{:S(2)}) copy-start(bf16[2,384]{1,0:T(2,128)(2,1)S(1)} %gather_fusion) | copy-start | bytes 4612
  55.2 45.2 %copy-start.37 = (f32[2,256]{1,0:T(2,128)}, f32[2,256]{1,0:T(2,128)S(1)}, u32[]{:S(2)}) copy-start(f32[2,256]{1,0:T(2,128)S(1)} %broadcast_multiply_fusion.2) | copy-start | bytes 6148
  55.5 21.5 %copy-start.45 = (f32[2,256]{1,0:T(2,128)}, f32[2,256]{1,0:T(2,128)S(1)}, u32[]{:S(2)}) copy-start(f32[2,256]{1,0:T(2,128)S(1)} %fusion.69) | copy-start | bytes 6148
  55.5 39.9 %copy-start.54 = (pred[2]{0:T(512)(128)(4,1)}, pred[2]{0:T(512)(128)(4,1)S(1)}, u32[]{:S(2)}) copy-start(pred[2]{0:T(512)(128)(4,1)S(1)} %compare_and_fusion) | copy-start | bytes 10
  55.5 44.9 %copy-start.47 = (f32[2,256]{1,0:T(2,128)}, f32[2,256]{1,0:T(2,128)S(1)}, u32[]{:S(2)}) copy-start(f32[2,256]{1,0:T(2,128)S(1)} %fusion.85) | copy-start | bytes 6148
  95.4 5.0 copy-start.25
  98.1 3.4 copy-start.40
  98.1 3.4 copy-start.42
  99.3 3.7 copy-start.11
  109.6 2.9 copy-start.20
  112.5 5.0 copy-start.5
  112.5 2.8 copy-start.32
  117.5 4.2 copy-start.35
  153.2 2.6 copy-start.53
  153.2 2.6 copy-start.59
  153.2 2.6 copy-start.58
  153.2 2.7 copy-start.52
  153.2 2.7 copy-start.50
  153.2 2.7 copy-start.55
  163.0 4.1 copy-start.14
  170.0 3.1 copy-start.19
  178.2 3.8 copy-start.10
  186.3 399.0 %all-gather.10.cloned.1.call-start = ((), (), s32[]{:S(2)}) async-start(), calls=%async_computation.2 | async-start | bytes 23887872 | tf_op jit(solution)/shard_map/all_gather | solution.py:215
  397.5 343.9 %all-gather.8.cloned.1.call-start = ((), (), s32[]{:S(2)}) async-start(), calls=%async_computation.1 | async-start | bytes 13271040 | tf_op jit(solution)/shard_map/all_gather | solution.py:217
  632.5 4.5 copy-start.7
  637.0 435.9 %all-reduce.7.cloned.1.call-start = ((), (), s32[]{:S(2)}) async-start(), calls=%async_computation.4 | async-start | bytes 21233664
  848.9 224.1 %copy-start.8 = (f32[663552]{0:T(1024)S(1)}, f32[663552]{0:T(1024)}, u32[]{:S(2)}) copy-start(f32[663552]{0:T(1024)} %param.19) | copy-start | bytes 7962628
  (32 other events, 47.5 us)
Sparse Core Ops, SparseCore 0:
  10.4 64.7 all-gather.5
  186.4 207.6 all-reduce.4
  397.6 187.5 all-gather.9
  637.2 104.1 all-gather.7
  849.0 223.9 all-reduce.6
